TPU v7x, 768 devices: a whole 4x8x12 slice. The times are simulated.
768 devices in a mesh: block: 32 (over y_lo, x, core), walker: 24 (over z, y_hi).
Axes of the slice: x: 4, y: 8 (y_hi: 2, y_lo: 4; y = y_hi * 4 + y_lo), z: 12, core: 2. Of those that a mesh axis runs over, the one named last changes fastest.
Arguments:
- green: bfloat16 [120, 294912], P('walker', 'block'), may hold values from -6 to 6
- chol: bfloat16 [256, 192, 1536], P('block'), may hold values from -0.15625 to 0.15625
- counts: int32 [24], replicated, may hold values from 1 to 5, as said below
- move_slot: int32 [24, 2], replicated, may hold values from -1 to 4, as said below
- move_dest: int32 [24, 2], replicated, may hold values from -1 to 23, as said below
Outputs:
- new_green: bfloat16 [72, 294912], P('walker', 'block')
- energy: float32 [72], P('walker')
Inputs may be any that keep to these rules, and one draw needn't show every extreme that they name: On every device, counts minus the walkers it sends plus the walkers it receives equals 3; in every draw some device has count 5 and some device has count 1. `move_slot`: in each row the entries >= 0 come first, are distinct, and name live slots of that device; the rest are -1. `move_dest`: -1 exactly where move_slot is -1, else another device's index; from one device at most 1 walker goes to any one device, and some device sends that many to one.
All inputs are finite; a program needn't handle non-finite values.
Results may differ from a plain program's by a relative error of at most 0.0004.
Values may be sent and summed in bfloat16 or wider, within the bound.
A program may use at most 32 MiB of HBM per device.

v0:
```python
import math

import jax
import jax.numpy as jnp
from jax import lax
from jax.sharding import PartitionSpec as P


def arrival_ranks(move_slot, move_dest):
    active = move_slot >= 0
    move_total = move_slot.shape[1]
    earlier = jnp.arange(move_total)[None, :] < jnp.arange(move_total)[:, None]
    same_target = (
        (move_dest[:, :, None] == move_dest[:, None, :]) & earlier[None, :, :] & active[:, None, :]
    )
    return (active, jnp.sum(same_target.astype(jnp.int32), axis=2))


def body(green, chol, counts, move_slot, move_dest):
    walker_total = lax.axis_size("walker")
    own_index = lax.axis_index("walker")
    slot_total = green.shape[0]
    share_width = green.shape[1]
    keep_total = slot_total - move_slot.shape[1]
    capacity = (move_slot.shape[1] + walker_total - 2) // (walker_total - 1)
    occ_count = chol.shape[1]
    orb_count = chol.shape[2]
    energy_scale = 0.5 / (occ_count * math.sqrt(chol.shape[0] * lax.axis_size("block")))
    active, move_rank = arrival_ranks(move_slot, move_dest)
    own_slots = move_slot[own_index]
    own_dests = move_dest[own_index]
    own_active = active[own_index]
    own_rank = move_rank[own_index]
    peer_ids = jnp.arange(walker_total)
    place_ids = jnp.arange(capacity)
    chosen = (
        (own_dests[None, None, :] == peer_ids[:, None, None])
        & (own_rank[None, None, :] == place_ids[None, :, None])
        & own_active[None, None, :]
    )
    send_slot = jnp.sum(jnp.where(chosen, own_slots[None, None, :], 0), axis=2).reshape(-1)
    present = jnp.any(chosen, axis=2).reshape(-1)
    arrive = jnp.any(
        (move_dest[:, None, :] == own_index)
        & (move_rank[:, None, :] == place_ids[None, :, None])
        & active[:, None, :],
        axis=2,
    ).reshape(-1)
    slot_ids = jnp.arange(slot_total)
    occupied = slot_ids < counts[own_index]
    leaving = jnp.any(own_slots[:, None] == slot_ids[None, :], axis=0)
    staying = occupied & jnp.logical_not(leaving)
    stay_rank = jnp.cumsum(staying.astype(jnp.int32)) - 1
    arrive_rank = jnp.cumsum(arrive.astype(jnp.int32)) - 1
    stay_total = jnp.sum(staying.astype(jnp.int32))
    targets = jnp.arange(keep_total)
    from_stay = jnp.sum(
        jnp.where(
            staying[None, :] & (stay_rank[None, :] == targets[:, None]), slot_ids[None, :], 0
        ),
        axis=1,
    )
    arrive_ids = jnp.arange(arrive.shape[0]) + slot_total
    from_arrive = jnp.sum(
        jnp.where(
            arrive[None, :] & (arrive_rank[None, :] == (targets - stay_total)[:, None]),
            arrive_ids[None, :],
            0,
        ),
        axis=1,
    )
    source_row = jnp.where(targets < stay_total, from_stay, from_arrive)
    outgoing = jnp.where(
        present[:, None], jnp.take(green, send_slot, axis=0), jnp.zeros((), jnp.bfloat16)
    )
    outgoing = outgoing.reshape(walker_total, capacity, share_width)

    def walker_energy(walker_row):
        green_mat = walker_row.reshape(occ_count, orb_count)
        transfer = jnp.einsum("gip,jp->gij", chol, green_mat, preferred_element_type=jnp.float32)
        return jnp.sum(transfer * jnp.swapaxes(transfer, 1, 2))

    complete = lax.all_gather(green, "block", axis=1, tiled=True)

    def slot_step(slot_index, totals):
        walker_row = lax.dynamic_index_in_dim(complete, slot_index, 0, keepdims=False)
        return totals.at[slot_index].set(walker_energy(walker_row))

    partial_value = lax.fori_loop(
        0, counts[own_index], slot_step, jnp.zeros((slot_total,), jnp.float32)
    )
    energy_here = -energy_scale * lax.psum(partial_value, "block")
    sent_energy = jnp.where(present, jnp.take(energy_here, send_slot), 0.0).reshape(
        walker_total, capacity
    )
    got_rows = lax.all_to_all(outgoing, "walker", split_axis=0, concat_axis=0, tiled=True)
    got_energy = lax.all_to_all(sent_energy, "walker", split_axis=0, concat_axis=0, tiled=True)
    source_pool = jnp.concatenate([green, got_rows.reshape(-1, share_width)], axis=0)
    energy_pool = jnp.concatenate([energy_here, got_energy.reshape(-1)], axis=0)
    new_green = jnp.take(source_pool, source_row, axis=0)
    energy = jnp.take(energy_pool, source_row)
    return (new_green, energy)


def solution(mesh):
    in_specs = (P("walker", "block"), P("block", None, None), P(), P(), P())
    out_specs = (P("walker", "block"), P("walker"))
    return jax.shard_map(body, mesh=mesh, in_specs=in_specs, out_specs=out_specs, check_vma=False)
```

profile of v0, /device:TPU:1, one launch (start us, length us, event | category | flops | bytes accessed | tf_op | source)
XLA Modules:
  0.0 278.9 jit_solution(9697444090185935745)
XLA Ops:
  13.3 1.0 reduce.19
  14.2 1.1 reshape.557
  15.3 21.2 %all-to-all-start = ((bf16[24,2,4608]{2,1,0:T(2,128)(2,1)}), bf16[24,2,4608]{2,1,0:T(2,128)(2,1)S(1)}, u32[]{:S(2)}, u32[]{:S(2)}) async-start(bf16[24,2,4608]{2,1,0:T(2,128)(2,1)} %reshape.557), calls=%async_computation | async-start | bytes 884736 | tf_op jit(solution)/shard_map/all_to_all | solution.py:96
  38.2 1.3 convert_reduce_fusion
  41.2 15.9 %all-to-all-done = bf16[24,2,4608]{2,1,0:T(2,128)(2,1)S(1)} async-done(((bf16[24,2,4608]{2,1,0:T(2,128)(2,1)}), bf16[24,2,4608]{2,1,0:T(2,128)(2,1)S(1)}, u32[]{:S(2)}, u32[]{:S(2)}) %all-to-all-start) | async-done | bytes 442400 | tf_op jit(solution)/shard_map/all_to_all | solution.py:96
  58.4 32.9 %all-gather.2.cloned.1.call-done = bf16[5,294912]{1,0:T(8,128)(2,1)} async-done(((bf16[5,9216]{1,0:T(8,128)(2,1)}), bf16[5,294912]{1,0:T(8,128)(2,1)}) %all-gather.2.cloned.1.call-update) | async-done | bytes 2949136 | tf_op jit(solution)/shard_map/all_gather | solution.py:83
  91.3 71.2 %while.11 = (s32[]{:T(128)}, f32[5]{0:T(128)S(1)}, s32[]{:T(128)}, bf16[5,294912]{1,0:T(8,128)(2,1)}, bf16[8,192,1536]{2,1,0:T(8,128)(2,1)}, /*index=5*/s32[]{:T(128)}, s32[]{:T(128)}, s32[]{:T(128)}, s32[]{:T(128)}) while((s32[]{:T(128)}, f32[5]{0:T(128)S(1)}, s32[]{:T(128)}, bf16[5,294912]{1,0:T(8,128)(2,1)}, ...), condition=%wide.region_12.13_spmd, body=%wide.region_10.12_spmd.sunk | while | flops 906559488 | bytes 13566165 | solution.py:89
  92.0 10.0 %dynamic-slice_reduce_fusion.5 = bf16[294912]{0:T(1024)(128)(2,1)S(1)} fusion(bf16[5,294912]{1,0:T(8,128)(2,1)} %get-tuple-element.112, s32[]{:T(128)S(6)} %select_n.207), kind=kLoop, calls=%fused_computation.6.clone.1 | loop fusion | bytes 1179652 | tf_op jit(solution)/shard_map/while/body/jit(dynamic_index_in_dim)/dynamic_slice | solution.py:86
  102.7 3.7 %fusion.17 = f32[192,8,192]{2,0,1:T(8,128)S(1)} fusion(bf16[192,1536,1]{1,0,2:T(8,128)(2,1)S(1)} %reshape.560, bf16[8,192,1536]{2,1,0:T(8,128)(2,1)} %get-tuple-element.113), kind=kOutput, calls=%fused_computation.57.clone.1 | convolution fusion | flops 905969664 | bytes 6488064 | tf_op jit(solution)/shard_map/while/body/gip,jp->gij/dot_general | solution.py:80
  107.0 1.1 fusion.18
  109.6 10.0 %dynamic-slice_reduce_fusion.5 = bf16[294912]{0:T(1024)(128)(2,1)S(1)} fusion(bf16[5,294912]{1,0:T(8,128)(2,1)} %get-tuple-element.112, s32[]{:T(128)S(6)} %select_n.207), kind=kLoop, calls=%fused_computation.6.clone.1 | loop fusion | bytes 1179652 | tf_op jit(solution)/shard_map/while/body/jit(dynamic_index_in_dim)/dynamic_slice | solution.py:86
  120.3 3.7 %fusion.17 = f32[192,8,192]{2,0,1:T(8,128)S(1)} fusion(bf16[192,1536,1]{1,0,2:T(8,128)(2,1)S(1)} %reshape.560, bf16[8,192,1536]{2,1,0:T(8,128)(2,1)} %get-tuple-element.113), kind=kOutput, calls=%fused_computation.57.clone.1 | convolution fusion | flops 905969664 | bytes 6488064 | tf_op jit(solution)/shard_map/while/body/gip,jp->gij/dot_general | solution.py:80
  124.7 1.1 fusion.18
  127.2 10.0 %dynamic-slice_reduce_fusion.5 = bf16[294912]{0:T(1024)(128)(2,1)S(1)} fusion(bf16[5,294912]{1,0:T(8,128)(2,1)} %get-tuple-element.112, s32[]{:T(128)S(6)} %select_n.207), kind=kLoop, calls=%fused_computation.6.clone.1 | loop fusion | bytes 1179652 | tf_op jit(solution)/shard_map/while/body/jit(dynamic_index_in_dim)/dynamic_slice | solution.py:86
  138.0 3.7 %fusion.17 = f32[192,8,192]{2,0,1:T(8,128)S(1)} fusion(bf16[192,1536,1]{1,0,2:T(8,128)(2,1)S(1)} %reshape.560, bf16[8,192,1536]{2,1,0:T(8,128)(2,1)} %get-tuple-element.113), kind=kOutput, calls=%fused_computation.57.clone.1 | convolution fusion | flops 905969664 | bytes 6488064 | tf_op jit(solution)/shard_map/while/body/gip,jp->gij/dot_general | solution.py:80
  142.3 1.1 fusion.18
  144.9 10.0 %dynamic-slice_reduce_fusion.5 = bf16[294912]{0:T(1024)(128)(2,1)S(1)} fusion(bf16[5,294912]{1,0:T(8,128)(2,1)} %get-tuple-element.112, s32[]{:T(128)S(6)} %select_n.207), kind=kLoop, calls=%fused_computation.6.clone.1 | loop fusion | bytes 1179652 | tf_op jit(solution)/shard_map/while/body/jit(dynamic_index_in_dim)/dynamic_slice | solution.py:86
  155.6 3.7 %fusion.17 = f32[192,8,192]{2,0,1:T(8,128)S(1)} fusion(bf16[192,1536,1]{1,0,2:T(8,128)(2,1)S(1)} %reshape.560, bf16[8,192,1536]{2,1,0:T(8,128)(2,1)} %get-tuple-element.113), kind=kOutput, calls=%fused_computation.57.clone.1 | convolution fusion | flops 905969664 | bytes 6488064 | tf_op jit(solution)/shard_map/while/body/gip,jp->gij/dot_general | solution.py:80
  160.0 1.1 fusion.18
  162.5 67.0 %psum.7 = f32[5]{0:T(128)S(1)} all-reduce(f32[5]{0:T(128)S(1)} %get-tuple-element.42), channel_id=1, replica_groups=mesh['block'=32,'walker'=24] {'block'}, use_global_device_ids=true, to_apply=%region_13.14 | all-reduce | flops 5 | bytes 40 | tf_op jit(solution)/shard_map/psum | solution.py:92
  231.0 24.8 %all-to-all-start.1 = ((f32[24,1,1]{2,1,0:T(1,128)}), f32[24,1,1]{2,1,0:T(1,128)S(1)}, u32[]{:S(2)}, u32[]{:S(2)}) async-start(f32[24,1,1]{2,1,0:T(1,128)} %copy.34), calls=%async_computation.1 | async-start | bytes 24576 | tf_op jit(solution)/shard_map/all_to_all | solution.py:97
  255.8 1.2 pad_maximum_fusion
  257.6 11.7 %all-to-all-done.1 = f32[24,1,1]{2,1,0:T(1,128)S(1)} async-done(((f32[24,1,1]{2,1,0:T(1,128)}), f32[24,1,1]{2,1,0:T(1,128)S(1)}, u32[]{:S(2)}, u32[]{:S(2)}) %all-to-all-start.1) | async-done | bytes 128 | tf_op jit(solution)/shard_map/all_to_all | solution.py:97
  270.2 1.1 broadcast_select_fusion.1
  (65 shorter events, 22.6 us)
Async XLA Ops:
  7.2 4.6 %copy-start = (bf16[5,9216]{1,0:T(8,128)(2,1)S(1)}, bf16[5,9216]{1,0:T(8,128)(2,1)}, u32[]{:S(2)}) copy-start(bf16[5,9216]{1,0:T(8,128)(2,1)} %param.9) | copy-start | bytes 276484
  7.2 84.1 %all-gather.2.cloned.1.call-start = ((), (), s32[]{:S(2)}) async-start(), calls=%async_computation.2 | async-start | bytes 4866048 | tf_op jit(solution)/shard_map/all_gather | solution.py:83
  12.6 23.9 %copy-start.3 = (s32[24]{0:T(128)S(1)}, s32[24]{0:T(128)}, u32[]{:S(2)}) copy-start(s32[24]{0:T(128)} %param.11) | copy-start | bytes 292
  12.6 24.5 %copy-start.1 = (s32[24,2]{0,1:T(2,128)S(1)}, s32[24,2]{0,1:T(2,128)}, u32[]{:S(2)}) copy-start(s32[24,2]{0,1:T(2,128)} %param.13) | copy-start | bytes 580
  12.6 24.5 %copy-start.2 = (s32[24,2]{0,1:T(2,128)S(1)}, s32[24,2]{0,1:T(2,128)}, u32[]{:S(2)}) copy-start(s32[24,2]{0,1:T(2,128)} %param.12) | copy-start | bytes 580
  15.3 41.7 %all-to-all-start = ((bf16[24,2,4608]{2,1,0:T(2,128)(2,1)}), bf16[24,2,4608]{2,1,0:T(2,128)(2,1)S(1)}, u32[]{:S(2)}, u32[]{:S(2)}) async-start(bf16[24,2,4608]{2,1,0:T(2,128)(2,1)} %reshape.557), calls=%async_computation | async-start | bytes 884736 | tf_op jit(solution)/shard_map/all_to_all | solution.py:96
  231.0 38.3 %all-to-all-start.1 = ((f32[24,1,1]{2,1,0:T(1,128)}), f32[24,1,1]{2,1,0:T(1,128)S(1)}, u32[]{:S(2)}, u32[]{:S(2)}) async-start(f32[24,1,1]{2,1,0:T(1,128)} %copy.34), calls=%async_computation.1 | async-start | bytes 24576 | tf_op jit(solution)/shard_map/all_to_all | solution.py:97
Sparse Core Ops, SparseCore 0:
  10.4 80.8 all-gather.1
where the time goes:
time: 281 us; the launch traced here: 279 us
  blocking collectives  67 us (24%)
  waiting for transfers between devices  61.1 us (22%)
  local copies, waits for them, and re-layouts  54.2 us (19%)
  starting transfers between devices  46 us (16%)
  other arithmetic  17.9 us (6%)
  matrix products  14.9 us (5%)
  between operations  14.2 us (5%)
  loops' own time  3.43 us (1%)
    psum x1, blocking collectives, body(): energy_here = -energy_scale * lax.psum(partial_value, 'block')  67 us
    dynamic_slice x4, local copies, waits for them, and re-layouts, slot_step(): lax.dynamic_index_in_dim(complete, slot_index, 0, keepdims=False)  40.2 us
    all_gather x1, waiting for transfers between devices, body(): complete = lax.all_gather(green, 'block', axis=1, tiled=True)  32.9 us
    all_to_all x1, starting transfers between devices, body(): lax.all_to_all(sent_energy, 'walker', split_axis=0, concat_axis=0, tiled=...  24.8 us
    all_to_all x1, starting transfers between devices, body(): lax.all_to_all(outgoing, 'walker', split_axis=0, concat_axis=0, tiled=True)  21.2 us
    all_to_all x1, waiting for transfers between devices, body(): lax.all_to_all(outgoing, 'walker', split_axis=0, concat_axis=0, tiled=True)  15.9 us
    dot_general x4, matrix products, walker_energy(): jnp.einsum('gip,jp->gij', chol, green_mat, preferred_element_type=jnp.flo...  14.9 us
    all_to_all x1, waiting for transfers between devices, body(): lax.all_to_all(sent_energy, 'walker', split_axis=0, concat_axis=0, tiled=...  11.7 us
  transfers between devices with their start and end apart: 3, of which 3 were waited for; matrix products, arithmetic and copies ran while one was open for 5% of the time, Pallas kernels for 0%

commit v1 on v0

v1 whole, which is shorter than its diff:
```python
import math

import jax
import jax.numpy as jnp
from jax import lax
from jax.experimental import pallas as pl
from jax.experimental.pallas import tpu as pltpu
from jax.sharding import PartitionSpec as P

MESH = pl.DeviceIdType.MESH
NT = (((1,), (1,)), ((), ()))
BF = jnp.bfloat16
F32 = jnp.float32
SLOTS = 5
KEEP = 3
X, Y, YH, Z = 4, 4, 2, 12
ROWS = 6
NORB = 1536
NOCC = 192
SHARE = ROWS * NORB
LINES = SHARE // 128


def trace_half(t):
    acc = jnp.zeros((64, 128), F32)
    corners = []
    for pair in range(2):
        t0 = t[:, 384 * pair : 384 * pair + 128]
        t1 = t[:, 384 * pair + 128 : 384 * pair + 256]
        t2 = t[:, 384 * pair + 256 : 384 * pair + 384]
        for a in (t0[0:128], t2[0:128]):
            m = a * a.T
            acc = acc + m[0:64] + m[64:128]
        b = t1[0:128].T
        acc = acc + 2.0 * (b[0:64] * t0[128:192] + b[64:128] * t2[128:192])
        corners.append(t1[128:192])
    e = jnp.concatenate(corners, 0)
    et = e.T
    low = lax.broadcasted_iota(jnp.int32, (64, 128), 1) < 64
    r0 = pltpu.roll(et[0:64], 64, 1)
    r1 = pltpu.roll(et[64:128], 64, 1)
    acc = acc + e[0:64] * jnp.where(low, et[0:64], r1)
    return acc + e[64:128] * jnp.where(low, r0, et[64:128])


def kernel(
    green, chol, counts, mslot, mdest, new_ref, en_ref,
    gin, x32, s32, g72, line, n32, gbuf, lbuf, xsend, xrecv, cbuf, gc, tbuf, ea, eb, ec,
    local_sem, send_sem, rg, rl, ra, rb, rc, rx,
):
    blk = lax.axis_index("block")
    wlk = lax.axis_index("walker")
    c = lax.rem(blk, 2)
    x = lax.rem(lax.div(blk, 2), X)
    y = lax.div(blk, 2 * X)
    yh = lax.rem(wlk, YH)
    z = lax.div(wlk, YH)
    oc = 1 - c
    xp, xm, xo = lax.rem(x + 1, X), lax.rem(x + X - 1, X), lax.rem(x + 2, X)
    ys = [y, y + 1 - 2 * lax.rem(y, 2), y + 2 - 4 * lax.div(y, 2), 3 - y]

    def shard(yy, xx, cc):
        return (yy * X + xx) * 2 + cc

    def dev(yy, xx, cc, zz, hh):
        return {"block": shard(yy, xx, cc), "walker": zz * YH + hh}

    def zat(offset):
        return lax.rem(z + offset + Z, Z)

    green_copy = pltpu.make_async_copy(green, gin, local_sem.at[0])
    green_copy.start()
    chol_copy = pltpu.make_async_copy(chol, cbuf, local_sem.at[1])
    chol_copy.start()

    xc_peers = [dev(y, lax.rem(x + dx, X), cc, z, yh) for dx in range(X) for cc in (c, oc)][1:]
    y_peers = [dev(ys[i], x, c, z, yh) for i in range(1, Y)]
    y_peers += [dev(ys[i], x, c, z, 1 - yh) for i in range(Y)]
    z_peers = [dev(y, x, c, zat(i), yh) for i in range(1, Z)]
    peers = xc_peers + y_peers + z_peers
    barrier = pltpu.get_barrier_semaphore()
    for peer in peers:
        pl.semaphore_signal(barrier, inc=1, device_id=peer, device_id_type=MESH)

    sent = []

    def send(src, dst, rsem, device):
        copy = pltpu.make_async_remote_copy(
            src_ref=src, dst_ref=dst, send_sem=send_sem.at[len(sent)], recv_sem=rsem,
            device_id=device, device_id_type=MESH,
        )
        copy.start()
        sent.append(copy)

    def arrive(dst, rsem, device):
        pltpu.make_async_remote_copy(
            src_ref=dst, dst_ref=dst, send_sem=send_sem.at[0], recv_sem=rsem,
            device_id=device, device_id_type=MESH,
        ).wait_recv()

    green_copy.wait()
    x32[0:SLOTS, :] = gin[...].astype(F32)
    s32[24:32, :] = jnp.zeros((8, NORB), F32)
    for r in range(ROWS):
        s32[SLOTS * r : SLOTS * r + SLOTS, :] = x32[0:SLOTS, NORB * r : NORB * r + NORB]
    gbuf[blk] = s32[...].astype(BF)

    for s in range(SLOTS):
        for r in range(LINES):
            g72[s, r : r + 1, :] = x32[s : s + 1, 128 * r : 128 * r + 128]
    for j in range(2):
        lbuf[z, j] = g72[jnp.maximum(mslot[wlk, j], 0)].astype(BF)

    partner = wlk + 1 - 2 * yh
    zero = jnp.int32(0)

    def scan(d, carry):
        own, n, other, m = carry
        for j in range(2):
            dest = mdest[d, j]
            live = mslot[d, j] >= 0
            hit = jnp.where(live & (dest == wlk), 1, 0)
            own = tuple(jnp.where((hit == 1) & (n == a), d * 2 + j, own[a]) for a in range(KEEP))
            n = n + hit
            hit = jnp.where(live & (dest == partner), 1, 0)
            other = tuple(jnp.where((hit == 1) & (m == a), d * 2 + j, other[a]) for a in range(KEEP))
            m = m + hit
        return own, n, other, m

    own, _, other, _ = lax.fori_loop(
        0, Z * YH, scan, ((zero,) * KEEP, zero, (zero,) * KEEP, zero)
    )
    stay_total = zero
    stay = [zero] * KEEP
    for s in range(SLOTS):
        hit = jnp.where((s < counts[wlk]) & (mslot[wlk, 0] != s) & (mslot[wlk, 1] != s), 1, 0)
        stay = [jnp.where((hit == 1) & (stay_total == t), s, stay[t]) for t in range(KEEP)]
        stay_total = stay_total + hit

    pl.semaphore_wait(barrier, len(peers))

    xpd, xmd, pd = dev(y, xp, c, z, yh), dev(y, xm, c, z, yh), dev(y, x, oc, z, yh)
    zpd, zmd = dev(y, x, c, zat(1), yh), dev(y, x, c, zat(-1), yh)

    def forward(i, first):
        b = shard(ys[i], x, c)
        if not first:
            arrive(gbuf.at[b], rg.at[b, 0], pd)
        send(gbuf.at[b], gbuf.at[b], rg.at[b, 0], xpd)
        send(gbuf.at[b], gbuf.at[b], rg.at[b, 0], xmd)
        if first:
            for k in range(1, Y):
                send(gbuf.at[b], gbuf.at[b], rg.at[b, 0], y_peers[k - 1])
        send(gbuf.at[b], gbuf.at[b], rg.at[b, 0], pd)

    def relay(i):
        b = shard(ys[i], xm, c)
        arrive(gbuf.at[b], rg.at[b, 0], pd)
        send(gbuf.at[b, 0:16], gbuf.at[b, 0:16], rg.at[b, 0], xpd)
        send(gbuf.at[b], gbuf.at[b], rg.at[b, 0], pd)
        b = shard(ys[i], xp, c)
        arrive(gbuf.at[b], rg.at[b, 0], pd)
        send(gbuf.at[b, 16:32], gbuf.at[b, 16:32], rg.at[b, 1], xmd)
        send(gbuf.at[b], gbuf.at[b], rg.at[b, 0], pd)

    def opposite(i):
        b = shard(ys[i], xo, c)
        arrive(gbuf.at[b, 0:16], rg.at[b, 0], pd)
        arrive(gbuf.at[b, 16:32], rg.at[b, 1], pd)
        send(gbuf.at[b], gbuf.at[b], rg.at[b, 0], pd)

    def other_core(i):
        for xx in (x, xm, xp, xo):
            b = shard(ys[i], xx, oc)
            arrive(gbuf.at[b], rg.at[b, 0], pd)

    def zsend(t):
        lo, hi = zat(-(t - 1)), zat(t - 1)
        if t < 6:
            send(lbuf.at[lo], lbuf.at[lo], rl.at[lo, 0], zpd)
            send(lbuf.at[hi], lbuf.at[hi], rl.at[hi, 0], zmd)
        else:
            send(lbuf.at[lo, 0], lbuf.at[lo, 0], rl.at[lo, 0], zpd)
            send(lbuf.at[hi, 1], lbuf.at[hi, 1], rl.at[hi, 1], zmd)

    def zstep(t):
        lo, hi = zat(-t), zat(t)
        if t < 6:
            arrive(lbuf.at[lo], rl.at[lo, 0], pd)
            arrive(lbuf.at[hi], rl.at[hi, 0], pd)
            zsend(t + 1)
        else:
            arrive(lbuf.at[lo, 0], rl.at[lo, 0], pd)
            arrive(lbuf.at[lo, 1], rl.at[lo, 1], pd)

    row_id = lax.broadcasted_iota(jnp.int32, (240, 256), 0)
    col_id = lax.broadcasted_iota(jnp.int32, (240, 256), 1)
    inner = jnp.bitwise_and(col_id, 31)
    rr = jnp.right_shift(inner * 13, 6)
    target = (inner - SLOTS * rr) * 48 + jnp.right_shift(col_id, 5) * ROWS + rr
    pick = jnp.where((row_id == target) & (inner < 30), 1.0, 0.0).astype(BF)

    def compute(i):
        base = ys[i] * 8
        a = gbuf[pl.ds(base, 8)].reshape(256, NORB)
        for kc in range(6):
            cols = slice(256 * kc, 256 * kc + 256)
            gc[:, cols] = jnp.dot(pick, a[:, cols], preferred_element_type=F32).astype(BF)
        rows = pl.ds(pl.multiple_of(ys[i] * 48, 16), 48)

        def half(h, _):
            g = 4 * h
            w = jnp.concatenate(
                [
                    cbuf[g], cbuf[g + 1, 128:192], cbuf[g + 1, 0:128],
                    cbuf[g + 2], cbuf[g + 3, 128:192], cbuf[g + 3, 0:128],
                ],
                0,
            )
            t = lax.dot_general(gc[...], w, NT, preferred_element_type=F32)
            for s in range(SLOTS):
                tbuf[h, s, rows, :] = t[48 * s : 48 * s + 48]
            return 0

        lax.fori_loop(0, 2, half, 0)

    forward(0, True)
    zsend(1)
    forward(1, False)
    relay(0)
    zstep(1)
    opposite(0)
    zstep(2)
    forward(2, False)
    relay(1)
    zstep(3)
    other_core(0)
    chol_copy.wait()
    compute(0)
    opposite(1)
    zstep(4)
    forward(3, False)
    relay(2)
    other_core(1)
    compute(1)
    zstep(5)
    opposite(2)
    relay(3)
    other_core(2)
    compute(2)
    zstep(6)
    for a in range(KEEP):
        xsend[a] = lbuf[lax.div(other[a], 4), lax.rem(other[a], 2)]
    opposite(3)
    send(xsend, xrecv, rx.at[0], dev(y, x, c, z, 1 - yh))
    other_core(3)
    compute(3)

    lane = lax.broadcasted_iota(jnp.int32, (1, 128), 1)

    def slot_trace(s, part):
        tot = trace_half(tbuf[0, s]) + trace_half(tbuf[1, s])
        value = jnp.sum(jnp.sum(tot, axis=0, keepdims=True), axis=1, keepdims=True)
        return jnp.where(lane == s, value, part)

    part = lax.fori_loop(0, SLOTS, slot_trace, jnp.zeros((1, 128), F32))

    def exchange(buf, sem, me, value, targets, sources):
        buf[me] = value
        for device in targets:
            send(buf.at[me], buf.at[me], sem.at[me], device)
        for src in sources:
            arrive(buf.at[src], sem.at[src], pd)

    exchange(
        ea, ra, x * 2 + c, part, xc_peers,
        [lax.rem(x + dx, X) * 2 + cc for dx in range(X) for cc in (c, oc)][1:],
    )
    total = ea[0]
    for i in range(1, 2 * X):
        total = total + ea[i]
    exchange(
        eb, rb, yh * Y + y, total, y_peers,
        [yh * Y + ys[i] for i in range(1, Y)] + [(1 - yh) * Y + ys[i] for i in range(Y)],
    )
    first = eb[0] + eb[1] + eb[2] + eb[3]
    second = eb[4] + eb[5] + eb[6] + eb[7]
    exchange(
        ec, rc, z, first + pltpu.roll(second, 8, 1), z_peers, [zat(i) for i in range(1, Z)]
    )

    arrive(xrecv, rx.at[0], pd)
    scale = 0.5 / (NOCC * math.sqrt(256.0))
    for t in range(KEEP):
        stays = t < stay_total
        rank = jnp.clip(t - stay_total, 0, KEEP - 1)
        pick_id = own[0]
        for a in range(1, KEEP):
            pick_id = jnp.where(rank == a, own[a], pick_id)
        src_z = lax.div(pick_id, 4)
        src_h = lax.rem(lax.div(pick_id, 2), 2)
        src_j = lax.rem(pick_id, 2)
        moved = jnp.where(src_h == yh, lbuf[src_z, src_j].astype(F32), xrecv[rank].astype(F32))
        line[t] = jnp.where(stays, g72[stay[t]], moved)
        for r in range(LINES):
            n32[t : t + 1, 128 * r : 128 * r + 128] = line[t, r : r + 1, :]
        from_z = jnp.where(stays, z, src_z)
        from_h = jnp.where(stays, yh, src_h)
        from_s = jnp.where(stays, stay[t], jnp.maximum(mslot[src_z * 2 + src_h, src_j], 0))
        row = ec[from_z]
        en_ref[t] = -scale * jnp.sum(jnp.where(lane == from_h * 8 + from_s, row, 0.0))
    new_ref[...] = n32[0:KEEP, :].astype(BF)

    for copy in sent:
        copy.wait_send()


def body(green, chol, counts, move_slot, move_dest):
    hbm = pl.BlockSpec(memory_space=pl.ANY)
    smem = pl.BlockSpec(memory_space=pltpu.SMEM)
    return pl.pallas_call(
        kernel,
        out_shape=(
            jax.ShapeDtypeStruct((KEEP, SHARE), BF),
            jax.ShapeDtypeStruct((KEEP,), F32),
        ),
        in_specs=[hbm, hbm, smem, smem, smem],
        out_specs=(pl.BlockSpec(memory_space=pltpu.VMEM), smem),
        scratch_shapes=[
            pltpu.VMEM((SLOTS, SHARE), BF),
            pltpu.VMEM((8, SHARE), F32),
            pltpu.VMEM((32, NORB), F32),
            pltpu.VMEM((SLOTS, LINES, 128), F32),
            pltpu.VMEM((KEEP, LINES, 128), F32),
            pltpu.VMEM((8, SHARE), F32),
            pltpu.VMEM((32, 32, NORB), BF),
            pltpu.VMEM((Z, 2, LINES, 128), BF),
            pltpu.VMEM((KEEP, LINES, 128), BF),
            pltpu.VMEM((KEEP, LINES, 128), BF),
            pltpu.VMEM((8, NOCC, NORB), BF),
            pltpu.VMEM((240, NORB), BF),
            pltpu.VMEM((2, SLOTS, NOCC, 768), F32),
            pltpu.VMEM((2 * X, 1, 128), F32),
            pltpu.VMEM((YH * Y, 1, 128), F32),
            pltpu.VMEM((Z, 1, 128), F32),
            pltpu.SemaphoreType.DMA((2,)),
            pltpu.SemaphoreType.DMA((80,)),
            pltpu.SemaphoreType.DMA((32, 2)),
            pltpu.SemaphoreType.DMA((Z, 2)),
            pltpu.SemaphoreType.DMA((2 * X,)),
            pltpu.SemaphoreType.DMA((YH * Y,)),
            pltpu.SemaphoreType.DMA((Z,)),
            pltpu.SemaphoreType.DMA((1,)),
        ],
        compiler_params=pltpu.CompilerParams(
            collective_id=0, has_side_effects=True, vmem_limit_bytes=60 << 20
        ),
        name="exchange_energy",
    )(green, chol, counts, move_slot, move_dest)


def solution(mesh):
    in_specs = (P("walker", "block"), P("block", None, None), P(), P(), P())
    out_specs = (P("walker", "block"), P("walker"))
    return jax.shard_map(body, mesh=mesh, in_specs=in_specs, out_specs=out_specs, check_vma=False)
```

time: 281 us -> 73.8 us (0.26)
  Pallas kernels: 0 us -> 67.2 us
  blocking collectives: 67 us -> 0 us
  waiting for transfers between devices: 61.1 us -> 0 us
  local copies, waits for them, and re-layouts: 54.2 us -> 5.44 us
  starting transfers between devices: 46 us -> 0 us
  other arithmetic: 17.9 us -> 0 us
  matrix products: 14.9 us -> 0 us
  between operations: 14.2 us -> 0.64 us
  loops' own time: 3.43 us -> 0 us
    pallas_call x0 -> x1, Pallas kernels: none -> 67.2 us  [body(): pl.pallas_call(kernel, out_shape=(jax.ShapeDtypeStruct((KEEP, SHARE), BF)...]
    psum x1 -> x0, blocking collectives: 67 us -> none  [body(): energy_here = -energy_scale * lax.psum(partial_value, 'block')]
    all_to_all x2 -> x0, starting transfers between devices: 46 us -> none  [the longest x1 24.8 us: body(): lax.all_to_all(sent_energy, 'walker', split_axis=0, concat_axis=0, tiled=...]
    dynamic_slice x8 -> x0, local copies, waits for them, and re-layouts: 42.7 us -> none  [the longest x4 40.2 us: slot_step(): lax.dynamic_index_in_dim(complete, slot_index, 0, keepdims=False)]
    all_gather x1 -> x0, waiting for transfers between devices: 32.9 us -> none  [body(): complete = lax.all_gather(green, 'block', axis=1, tiled=True)]
    all_to_all x2 -> x0, waiting for transfers between devices: 27.5 us -> none  [the longest x1 15.9 us: body(): lax.all_to_all(outgoing, 'walker', split_axis=0, concat_axis=0, tiled=True)]
    dot_general x4 -> x0, matrix products: 14.9 us -> none  [walker_energy(): jnp.einsum('gip,jp->gij', chol, green_mat, preferred_element_type=jnp.flo...]
    reduce_sum x9 -> x0, other arithmetic: 6.95 us -> none  [the longest x4 4.41 us: walker_energy(): return jnp.sum(transfer * jnp.swapaxes(transfer, 1, 2))]
  transfers between devices with their start and end apart: 3 -> 0, of which waited for: 3 -> 0; matrix products, arithmetic and copies ran while one was open for 5% -> 0% of each run, Pallas kernels for 0% -> 0%
where the time goes in v1:
time: 73.8 us; the launch traced here: 73.3 us
  Pallas kernels  67.2 us (91%)
  local copies, waits for them, and re-layouts  5.44 us (7%)
    pallas_call x1, Pallas kernels, body(): pl.pallas_call(kernel, out_shape=(jax.ShapeDtypeStruct((KEEP, SHARE), BF)...  67.2 us
    unnamed x4, local copies, waits for them, and re-layouts  5.44 us

profile of v1, /device:TPU:1, one launch (start us, length us, event | category | flops | bytes accessed | tf_op | source)
XLA Modules:
  0.0 73.3 jit_solution(15874975562980379492)
XLA Ops:
  0.6 1.4 %copy.7.mslot = s32[24,2]{1,0:T(8,128)} copy(s32[24,2]{0,1:T(2,128)} %param.8) | data formatting | bytes 384 | tf_op args[3]
  2.0 1.4 %copy.8.mdest = s32[24,2]{1,0:T(8,128)} copy(s32[24,2]{0,1:T(2,128)} %param.9) | data formatting | bytes 384 | tf_op args[4]
  3.3 67.2 %exchange_energy.1 = (bf16[3,9216]{1,0:T(4,128)(2,1)}, f32[3]{0:T(128)}) custom-call(bf16[5,9216]{1,0:T(8,128)(2,1)} %green.1, bf16[8,192,1536]{2,1,0:T(8,128)(2,1)} %chol.1, s32[24]{0:T(128)} %counts.1, s32[24,2]{1,0:T(8,128)} %copy.7.mslot, s32[24,2]{1,0:T(8,128)} %copy.8.mdest), custom_call_target="tpu_custom_call" | custom-call | tf_op jit(solution)/shard_map/exchange_energy/pallas_call | solution.py:321
  70.5 1.5 %copy.11 = bf16[3,9216]{1,0:T(4,128)(2,1)} copy(bf16[3,9216]{1,0:T(4,128)(2,1)} %get-tuple-element.4) | data formatting | bytes 110592
  72.1 1.2 %copy.12 = f32[3]{0:T(128)} copy(f32[3]{0:T(128)} %get-tuple-element.5) | data formatting | bytes 24

commit v2 on v1

v2 whole, which is shorter than its diff:
```python
import math

import jax
import jax.numpy as jnp
from jax import lax
from jax.experimental import pallas as pl
from jax.experimental.pallas import tpu as pltpu
from jax.sharding import PartitionSpec as P

MESH = pl.DeviceIdType.MESH
NT = (((1,), (1,)), ((), ()))
BF = jnp.bfloat16
F32 = jnp.float32
SLOTS = 5
KEEP = 3
X, Y, YH, Z = 4, 4, 2, 12
ROWS = 6
NORB = 1536
NOCC = 192
SHARE = ROWS * NORB
LINES = SHARE // 128


def trace_half(t):
    acc = jnp.zeros((64, 128), F32)
    corners = []
    for pair in range(2):
        t0 = t[:, 384 * pair : 384 * pair + 128]
        t1 = t[:, 384 * pair + 128 : 384 * pair + 256]
        t2 = t[:, 384 * pair + 256 : 384 * pair + 384]
        for a in (t0[0:128], t2[0:128]):
            m = a * a.T
            acc = acc + m[0:64] + m[64:128]
        b = t1[0:128].T
        acc = acc + 2.0 * (b[0:64] * t0[128:192] + b[64:128] * t2[128:192])
        corners.append(t1[128:192])
    e = jnp.concatenate(corners, 0)
    et = e.T
    low = lax.broadcasted_iota(jnp.int32, (64, 128), 1) < 64
    r0 = pltpu.roll(et[0:64], 64, 1)
    r1 = pltpu.roll(et[64:128], 64, 1)
    acc = acc + e[0:64] * jnp.where(low, et[0:64], r1)
    return acc + e[64:128] * jnp.where(low, r0, et[64:128])


def kernel(
    green, chol, counts, mslot, mdest, new_ref, en_ref,
    gin, x32, s32, g72, line, n32, nout, gbuf, lbuf, xsend, xrecv, cbuf, gc, tbuf, ea, eb, ec,
    local_sem, send_sem, rg, rl, ra, rb, rc, rx, hyz,
):
    blk = lax.axis_index("block")
    wlk = lax.axis_index("walker")
    c = lax.rem(blk, 2)
    x = lax.rem(lax.div(blk, 2), X)
    y = lax.div(blk, 2 * X)
    yh = lax.rem(wlk, YH)
    z = lax.div(wlk, YH)
    oc = 1 - c
    xp, xm, xo = lax.rem(x + 1, X), lax.rem(x + X - 1, X), lax.rem(x + 2, X)
    y1 = y - 1 + 2 * lax.div(Y - y, Y)
    y3 = (Y - 1) * (1 - lax.div(y, 2))
    ys = [y, y1, 6 - y - y1 - y3, y3]

    def shard(yy, xx, cc):
        return (yy * X + xx) * 2 + cc

    def dev(yy, xx, cc, zz, hh):
        return {"block": shard(yy, xx, cc), "walker": zz * YH + hh}

    def zat(offset):
        return lax.rem(z + offset + Z, Z)

    green_copy = pltpu.make_async_copy(green, gin, local_sem.at[0])
    green_copy.start()
    chol_copy = pltpu.make_async_copy(chol, cbuf, local_sem.at[1])
    chol_copy.start()

    y8 = yh * Y + y

    def ydev(offset):
        at = lax.rem(y8 + offset + YH * Y, YH * Y)
        return dev(lax.rem(at, Y), x, c, z, lax.div(at, Y))

    xc_peers = [dev(y, lax.rem(x + dx, X), cc, z, yh) for dx in range(X) for cc in (c, oc)][1:]
    y_peers = [ydev(i) for i in range(1, YH * Y)]
    z_peers = [dev(y, x, c, zat(i), yh) for i in range(1, Z)]
    xpd, xmd, pd = dev(y, xp, c, z, yh), dev(y, xm, c, z, yh), dev(y, x, oc, z, yh)
    ypd, ymd = ydev(1), ydev(-1)
    zpd, zmd = dev(y, x, c, zat(1), yh), dev(y, x, c, zat(-1), yh)
    near = [xpd, xmd, pd, ypd, ymd, zpd, zmd]
    barrier = pltpu.get_barrier_semaphore()
    for peer in near:
        pl.semaphore_signal(barrier, inc=1, device_id=peer, device_id_type=MESH)

    sent = []

    def send(src, dst, rsem, device, cond=None):
        index = len(sent)

        def make():
            return pltpu.make_async_remote_copy(
                src_ref=src(), dst_ref=dst(), send_sem=send_sem.at[index], recv_sem=rsem(),
                device_id=device, device_id_type=MESH,
            )

        sent.append((make, cond))
        if cond is None:
            make().start()
        else:
            pl.when(cond)(lambda: make().start())

    def both(ref, rsem, device, cond=None):
        send(ref, ref, rsem, device, cond)

    def arrive(dst, rsem, device):
        pltpu.make_async_remote_copy(
            src_ref=dst, dst_ref=dst, send_sem=send_sem.at[0], recv_sem=rsem,
            device_id=device, device_id_type=MESH,
        ).wait_recv()

    green_copy.wait()
    x32[0:SLOTS, :] = gin[...].astype(F32)
    s32[24:32, :] = jnp.zeros((8, NORB), F32)
    for r in range(ROWS):
        s32[SLOTS * r : SLOTS * r + SLOTS, :] = x32[0:SLOTS, NORB * r : NORB * r + NORB]
    gbuf[blk] = s32[...].astype(BF)

    pl.semaphore_wait(barrier, len(near))

    def half(b, h):
        return lambda: gbuf.at[b, 16 * h : 16 * h + 16]

    def whole(b):
        return lambda: gbuf.at[b]

    def sem(b, h):
        return lambda: rg.at[b, h]

    def forward(i):
        b = shard(ys[i], x, c)
        if i == 0:
            up, down = y < Y - 1, y > 0
        else:
            up, down = (ys[i] < y) & (y < Y - 1), (ys[i] > y) & (y > 0)
        for h in range(2):
            if i > 0:
                arrive(gbuf.at[b, 16 * h : 16 * h + 16], rg.at[b, h], pd)
            both(half(b, h), sem(b, h), ypd, up)
            both(half(b, h), sem(b, h), ymd, down)
            both(half(b, h), sem(b, h), xpd)
        for h in (1, 0):
            both(half(b, h), sem(b, h), xmd)
        both(whole(b), sem(b, 0), pd)

    def relay(i):
        b = shard(ys[i], xm, c)
        arrive(gbuf.at[b, 0:16], rg.at[b, 0], pd)
        both(half(b, 0), sem(b, 0), xpd)
        b = shard(ys[i], xp, c)
        arrive(gbuf.at[b, 16:32], rg.at[b, 1], pd)
        both(half(b, 1), sem(b, 1), xmd)

    def rest(i):
        b = shard(ys[i], xm, c)
        arrive(gbuf.at[b, 16:32], rg.at[b, 1], pd)
        both(whole(b), sem(b, 0), pd)
        b = shard(ys[i], xp, c)
        arrive(gbuf.at[b, 0:16], rg.at[b, 0], pd)
        both(whole(b), sem(b, 0), pd)
        b = shard(ys[i], xo, c)
        arrive(gbuf.at[b, 0:16], rg.at[b, 0], pd)
        arrive(gbuf.at[b, 16:32], rg.at[b, 1], pd)
        both(whole(b), sem(b, 0), pd)

    def other_core(i):
        for xx in (x, xm, xp, xo):
            b = shard(ys[i], xx, oc)
            arrive(gbuf.at[b], rg.at[b, 0], pd)

    def zsend():
        for device in z_peers:
            both(lambda: lbuf.at[z], lambda: rl.at[z], device)

    def zarrive():
        for i in range(1, Z):
            arrive(lbuf.at[zat(i)], rl.at[zat(i)], pd)

    def hello(i):
        for device in (ypd, ymd, zpd, zmd):
            pl.semaphore_signal(hyz.at[i], inc=1, device_id=device, device_id_type=MESH)

    def heard(i):
        pl.semaphore_wait(hyz.at[i], 4)

    forward(0)
    hello(0)

    for s in range(SLOTS):
        for r in range(LINES):
            g72[s, r : r + 1, :] = x32[s : s + 1, 128 * r : 128 * r + 128]
    for j in range(2):
        lbuf[z, j] = g72[jnp.maximum(mslot[j, wlk], 0)].astype(BF)

    partner = wlk + 1 - 2 * yh
    zero = jnp.int32(0)

    def scan(d, carry):
        own, n, other, m = carry
        for j in range(2):
            dest = mdest[j, d]
            live = mslot[j, d] >= 0
            hit = jnp.where(live & (dest == wlk), 1, 0)
            own = tuple(jnp.where((hit == 1) & (n == a), d * 2 + j, own[a]) for a in range(KEEP))
            n = n + hit
            hit = jnp.where(live & (dest == partner), 1, 0)
            other = tuple(jnp.where((hit == 1) & (m == a), d * 2 + j, other[a]) for a in range(KEEP))
            m = m + hit
        return own, n, other, m

    own, _, other, _ = lax.fori_loop(
        0, Z * YH, scan, ((zero,) * KEEP, zero, (zero,) * KEEP, zero)
    )
    stay_total = zero
    stay = [zero] * KEEP
    for s in range(SLOTS):
        hit = jnp.where((s < counts[wlk]) & (mslot[0, wlk] != s) & (mslot[1, wlk] != s), 1, 0)
        stay = [jnp.where((hit == 1) & (stay_total == t), s, stay[t]) for t in range(KEEP)]
        stay_total = stay_total + hit

    row_id = lax.broadcasted_iota(jnp.int32, (240, 256), 0)
    col_id = lax.broadcasted_iota(jnp.int32, (240, 256), 1)
    inner = jnp.bitwise_and(col_id, 31)
    rr = jnp.right_shift(inner * 13, 6)
    target = (inner - SLOTS * rr) * 48 + jnp.right_shift(col_id, 5) * ROWS + rr
    pick = jnp.where((row_id == target) & (inner < 30), 1.0, 0.0).astype(BF)

    def gather_rows(i):
        a = gbuf[pl.ds(ys[i] * 8, 8)].reshape(256, NORB)
        for kc in range(6):
            cols = slice(256 * kc, 256 * kc + 256)
            gc[:, cols] = jnp.dot(pick, a[:, cols], preferred_element_type=F32).astype(BF)

    def multiply(i, h):
        rows = pl.ds(pl.multiple_of(ys[i] * 48, 16), 48)
        g = 4 * h
        w = jnp.concatenate(
            [
                cbuf[g], cbuf[g + 1, 128:192], cbuf[g + 1, 0:128],
                cbuf[g + 2], cbuf[g + 3, 128:192], cbuf[g + 3, 0:128],
            ],
            0,
        )
        t = lax.dot_general(gc[...], w, NT, preferred_element_type=F32)
        for s in range(SLOTS):
            tbuf[h, s, rows, :] = t[48 * s : 48 * s + 48]

    heard(0)
    hello(1)
    forward(1)
    heard(1)
    hello(2)
    relay(0)
    heard(2)
    hello(3)
    rest(0)
    heard(3)
    hello(4)
    forward(2)
    heard(4)
    zsend()
    relay(1)
    other_core(0)
    chol_copy.wait()
    gather_rows(0)
    rest(1)
    multiply(0, 0)
    forward(3)
    multiply(0, 1)
    relay(2)
    other_core(1)
    gather_rows(1)
    rest(2)
    multiply(1, 0)
    relay(3)
    multiply(1, 1)
    other_core(2)
    gather_rows(2)
    rest(3)
    multiply(2, 0)
    multiply(2, 1)
    zarrive()
    for a in range(KEEP):
        xsend[a] = lbuf[lax.div(other[a], 4), lax.rem(other[a], 2)]
    other_core(3)
    gather_rows(3)
    send(lambda: xsend, lambda: xrecv, lambda: rx.at[0], dev(y, x, c, z, 1 - yh))
    multiply(3, 0)
    multiply(3, 1)

    lane = lax.broadcasted_iota(jnp.int32, (1, 128), 1)
    part = jnp.zeros((1, 128), F32)
    tots = [trace_half(tbuf[0, s]) for s in range(SLOTS)]
    for s in range(SLOTS):
        tot = tots[s] + trace_half(tbuf[1, s])
        value = jnp.sum(jnp.sum(tot, axis=0, keepdims=True), axis=1, keepdims=True)
        part = jnp.where(lane == s, value, part)

    def exchange(buf, sem, me, value, targets, sources):
        buf[me] = value
        for device in targets:
            both(lambda: buf.at[me], lambda: sem.at[me], device)
        for src in sources:
            arrive(buf.at[src], sem.at[src], pd)

    exchange(
        ea, ra, x * 2 + c, part, xc_peers,
        [lax.rem(x + dx, X) * 2 + cc for dx in range(X) for cc in (c, oc)][1:],
    )
    total = ea[0]
    for i in range(1, 2 * X):
        total = total + ea[i]
    exchange(
        eb, rb, y8, total, y_peers,
        [lax.rem(y8 + i, YH * Y) for i in range(1, YH * Y)],
    )
    first = eb[0] + eb[1] + eb[2] + eb[3]
    second = eb[4] + eb[5] + eb[6] + eb[7]
    row = first + pltpu.roll(second, 8, 1)
    ec[z] = row
    for device in z_peers:
        both(lambda: ec.at[z], lambda: rc.at[z], device)

    arrive(xrecv, rx.at[0], pd)
    scale = 0.5 / (NOCC * math.sqrt(256.0))
    found = []
    for t in range(KEEP):
        stays = t < stay_total
        rank = jnp.clip(t - stay_total, 0, KEEP - 1)
        pick_id = own[0]
        for a in range(1, KEEP):
            pick_id = jnp.where(rank == a, own[a], pick_id)
        src_z = lax.div(pick_id, 4)
        src_h = lax.rem(lax.div(pick_id, 2), 2)
        src_j = lax.rem(pick_id, 2)
        moved = jnp.where(src_h == yh, lbuf[src_z, src_j].astype(F32), xrecv[rank].astype(F32))
        line[t] = jnp.where(stays, g72[stay[t]], moved)
        for r in range(LINES):
            n32[t : t + 1, 128 * r : 128 * r + 128] = line[t, r : r + 1, :]
        from_z = jnp.where(stays, z, src_z)
        from_h = jnp.where(stays, yh, src_h)
        from_s = jnp.where(stays, stay[t], jnp.maximum(mslot[src_j, src_z * 2 + src_h], 0))
        found.append((from_z, from_h * 8 + from_s))
    nout[...] = n32[0:KEEP, :].astype(BF)
    new_copy = pltpu.make_async_copy(nout, new_ref, local_sem.at[2])
    new_copy.start()
    for i in range(1, Z):
        arrive(ec.at[zat(i)], rc.at[zat(i)], pd)
    for t, (from_z, at) in enumerate(found):
        en_ref[t] = -scale * jnp.sum(jnp.where(lane == at, ec[from_z], 0.0))
    new_copy.wait()

    for make, cond in sent:
        if cond is None:
            make().wait_send()
        else:
            pl.when(cond)(lambda make=make: make().wait_send())


def body(green, chol, counts, move_slot, move_dest):
    hbm = pl.BlockSpec(memory_space=pl.ANY)
    smem = pl.BlockSpec(memory_space=pltpu.SMEM)
    return pl.pallas_call(
        kernel,
        out_shape=(
            jax.ShapeDtypeStruct((KEEP, SHARE), BF),
            jax.ShapeDtypeStruct((KEEP,), F32),
        ),
        in_specs=[hbm, hbm, smem, smem, smem],
        out_specs=(hbm, smem),
        scratch_shapes=[
            pltpu.VMEM((SLOTS, SHARE), BF),
            pltpu.VMEM((8, SHARE), F32),
            pltpu.VMEM((32, NORB), F32),
            pltpu.VMEM((SLOTS, LINES, 128), F32),
            pltpu.VMEM((KEEP, LINES, 128), F32),
            pltpu.VMEM((8, SHARE), F32),
            pltpu.VMEM((KEEP, SHARE), BF),
            pltpu.VMEM((32, 32, NORB), BF),
            pltpu.VMEM((Z, 2, LINES, 128), BF),
            pltpu.VMEM((KEEP, LINES, 128), BF),
            pltpu.VMEM((KEEP, LINES, 128), BF),
            pltpu.VMEM((8, NOCC, NORB), BF),
            pltpu.VMEM((240, NORB), BF),
            pltpu.VMEM((2, SLOTS, NOCC, 768), F32),
            pltpu.VMEM((2 * X, 1, 128), F32),
            pltpu.VMEM((YH * Y, 1, 128), F32),
            pltpu.VMEM((Z, 1, 128), F32),
            pltpu.SemaphoreType.DMA((3,)),
            pltpu.SemaphoreType.DMA((120,)),
            pltpu.SemaphoreType.DMA((32, 2)),
            pltpu.SemaphoreType.DMA((Z,)),
            pltpu.SemaphoreType.DMA((2 * X,)),
            pltpu.SemaphoreType.DMA((YH * Y,)),
            pltpu.SemaphoreType.DMA((Z,)),
            pltpu.SemaphoreType.DMA((1,)),
            pltpu.SemaphoreType.REGULAR((5,)),
        ],
        compiler_params=pltpu.CompilerParams(
            collective_id=0, has_side_effects=True, vmem_limit_bytes=60 << 20
        ),
        name="exchange_energy",
    )(green, chol, counts, move_slot.T, move_dest.T)


def solution(mesh):
    in_specs = (P("walker", "block"), P("block", None, None), P(), P(), P())
    out_specs = (P("walker", "block"), P("walker"))
    return jax.shard_map(body, mesh=mesh, in_specs=in_specs, out_specs=out_specs, check_vma=False)
```

time: 73.8 us -> 68.8 us (0.932)
  local copies, waits for them, and re-layouts: 5.44 us -> 2.65 us
  Pallas kernels: 67.2 us -> 65.3 us
    unnamed x4 -> x2, local copies, waits for them, and re-layouts: 5.44 us -> 2.65 us
    pallas_call x1, Pallas kernels: 67.2 us -> 65.3 us  [body(): pl.pallas_call(kernel, out_shape=(jax.ShapeDtypeStruct((KEEP, SHARE), BF)...]
where the time goes in v2:
time: 68.8 us; the launch traced here: 68.6 us
  Pallas kernels  65.3 us (95%)
  local copies, waits for them, and re-layouts  2.65 us (4%)
    pallas_call x1, Pallas kernels, body(): pl.pallas_call(kernel, out_shape=(jax.ShapeDtypeStruct((KEEP, SHARE), BF)...  65.3 us
    unnamed x2, local copies, waits for them, and re-layouts  2.65 us

profile of v2, /device:TPU:1, one launch (start us, length us, event | category | flops | bytes accessed | tf_op | source)
XLA Modules:
  0.0 68.6 jit_solution(3451431661976990551)
XLA Ops:
  0.6 65.3 %exchange_energy.1 = (bf16[3,9216]{1,0:T(4,128)(2,1)}, f32[3]{0:T(128)}) custom-call(bf16[5,9216]{1,0:T(8,128)(2,1)} %green.1, bf16[8,192,1536]{2,1,0:T(8,128)(2,1)} %chol.1, s32[24]{0:T(128)} %counts.1, s32[2,24]{1,0:T(2,128)} %bitcast.2, s32[2,24]{1,0:T(2,128)} %bitcast.3), custom_call_target="tpu_custom_call" | custom-call | tf_op jit(solution)/shard_map/exchange_energy/pallas_call | solution.py:372
  66.0 1.5 %copy.9 = bf16[3,9216]{1,0:T(4,128)(2,1)} copy(bf16[3,9216]{1,0:T(4,128)(2,1)} %get-tuple-element.4) | data formatting | bytes 110592
  67.5 1.1 %copy.10 = f32[3]{0:T(128)} copy(f32[3]{0:T(128)} %get-tuple-element.5) | data formatting | bytes 24

commit v3 on v2

--- a/solution.py
+++ b/solution.py
@@ -81,9 +81,9 @@
         at = lax.rem(y8 + offset + YH * Y, YH * Y)
         return dev(lax.rem(at, Y), x, c, z, lax.div(at, Y))
 
-    xc_peers = [dev(y, lax.rem(x + dx, X), cc, z, yh) for dx in range(X) for cc in (c, oc)][1:]
-    y_peers = [ydev(i) for i in range(1, YH * Y)]
-    z_peers = [dev(y, x, c, zat(i), yh) for i in range(1, Z)]
+    xc_peers = [dev(y, lax.rem(x + dx, X), cc, z, yh) for dx in (2, 1, 3, 0) for cc in (oc, c)][:7]
+    y_peers = [ydev(i) for i in (4, 3, 5, 2, 6, 1, 7)]
+    z_peers = [dev(y, x, c, zat(i), yh) for i in (6, 5, 7, 4, 8, 3, 9, 2, 10, 1, 11)]
     xpd, xmd, pd = dev(y, xp, c, z, yh), dev(y, xm, c, z, yh), dev(y, x, oc, z, yh)
     ypd, ymd = ydev(1), ydev(-1)
     zpd, zmd = dev(y, x, c, zat(1), yh), dev(y, x, c, zat(-1), yh)
@@ -136,21 +136,26 @@
     def sem(b, h):
         return lambda: rg.at[b, h]
 
-    def forward(i):
+    def forward(i, cond=None):
         b = shard(ys[i], x, c)
         if i == 0:
             up, down = y < Y - 1, y > 0
         else:
             up, down = (ys[i] < y) & (y < Y - 1), (ys[i] > y) & (y > 0)
+        if cond is not None:
+            up, down = up & cond, down & cond
         for h in range(2):
-            if i > 0:
-                arrive(gbuf.at[b, 16 * h : 16 * h + 16], rg.at[b, h], pd)
+            part = gbuf.at[b, 16 * h : 16 * h + 16]
+            if i > 0 and cond is None:
+                arrive(part, rg.at[b, h], pd)
+            elif i > 0:
+                pl.when(cond)(lambda: arrive(part, rg.at[b, h], pd))
             both(half(b, h), sem(b, h), ypd, up)
             both(half(b, h), sem(b, h), ymd, down)
-            both(half(b, h), sem(b, h), xpd)
+            both(half(b, h), sem(b, h), xpd, cond)
         for h in (1, 0):
-            both(half(b, h), sem(b, h), xmd)
-        both(whole(b), sem(b, 0), pd)
+            both(half(b, h), sem(b, h), xmd, cond)
+        both(whole(b), sem(b, 0), pd, cond)
 
     def relay(i):
         b = shard(ys[i], xm, c)
@@ -254,9 +259,11 @@
         for s in range(SLOTS):
             tbuf[h, s, rows, :] = t[48 * s : 48 * s + 48]
 
+    inside, edge = (y > 0) & (y < Y - 1), (y == 0) | (y == Y - 1)
     heard(0)
     hello(1)
     forward(1)
+    forward(2, inside)
     heard(1)
     hello(2)
     relay(0)
@@ -265,18 +272,19 @@
     rest(0)
     heard(3)
     hello(4)
-    forward(2)
+    forward(2, edge)
+    forward(3, inside)
     heard(4)
+    relay(1)
     zsend()
-    relay(1)
     other_core(0)
     chol_copy.wait()
     gather_rows(0)
     rest(1)
     multiply(0, 0)
-    forward(3)
+    forward(3, edge)
+    relay(2)
     multiply(0, 1)
-    relay(2)
     other_core(1)
     gather_rows(1)
     rest(2)
@@ -366,10 +374,16 @@
             pl.when(cond)(lambda make=make: make().wait_send())
 
 
+def finish(new_in, en_in, new_out, en_out):
+    new_out[...] = new_in[...]
+    for t in range(KEEP):
+        en_out[t] = en_in[t]
+
+
 def body(green, chol, counts, move_slot, move_dest):
     hbm = pl.BlockSpec(memory_space=pl.ANY)
     smem = pl.BlockSpec(memory_space=pltpu.SMEM)
-    return pl.pallas_call(
+    new, energy = pl.pallas_call(
         kernel,
         out_shape=(
             jax.ShapeDtypeStruct((KEEP, SHARE), BF),
@@ -396,7 +410,7 @@
             pltpu.VMEM((YH * Y, 1, 128), F32),
             pltpu.VMEM((Z, 1, 128), F32),
             pltpu.SemaphoreType.DMA((3,)),
-            pltpu.SemaphoreType.DMA((120,)),
+            pltpu.SemaphoreType.DMA((140,)),
             pltpu.SemaphoreType.DMA((32, 2)),
             pltpu.SemaphoreType.DMA((Z,)),
             pltpu.SemaphoreType.DMA((2 * X,)),
@@ -410,6 +424,17 @@
         ),
         name="exchange_energy",
     )(green, chol, counts, move_slot.T, move_dest.T)
+    vmem = pl.BlockSpec(memory_space=pltpu.VMEM)
+    return pl.pallas_call(
+        finish,
+        out_shape=(
+            jax.ShapeDtypeStruct((KEEP, SHARE), BF),
+            jax.ShapeDtypeStruct((KEEP,), F32),
+        ),
+        in_specs=[vmem, smem],
+        out_specs=(vmem, smem),
+        name="finish",
+    )(new, energy)
 
 
 def solution(mesh):

time: 68.8 us -> 65.7 us (0.955)
  local copies, waits for them, and re-layouts: 2.65 us -> 0 us
  Pallas kernels: 65.3 us -> 64.4 us
    unnamed x2 -> x0, local copies, waits for them, and re-layouts: 2.65 us -> none
    pallas_call x1, Pallas kernels: 65.3 us -> 62.8 us  [body(): pl.pallas_call(kernel, out_shape=(jax.ShapeDtypeStruct((KEEP, SHARE), BF)...]
    pallas_call x0 -> x1, Pallas kernels: none -> 1.55 us  [body(): pl.pallas_call(finish, out_shape=(jax.ShapeDtypeStruct((KEEP, SHARE), BF)...]
where the time goes in v3:
time: 65.7 us; the launch traced here: 65 us
  Pallas kernels  64.4 us (98%)
    pallas_call x1, Pallas kernels, body(): pl.pallas_call(kernel, out_shape=(jax.ShapeDtypeStruct((KEEP, SHARE), BF)...  62.8 us
    pallas_call x1, Pallas kernels, body(): pl.pallas_call(finish, out_shape=(jax.ShapeDtypeStruct((KEEP, SHARE), BF)...  1.55 us

profile of v3, /device:TPU:1, one launch (start us, length us, event | category | flops | bytes accessed | tf_op | source)
XLA Modules:
  0.0 65.0 jit_solution(17092159168883974245)
XLA Ops:
  0.6 62.8 %exchange_energy.1 = (bf16[3,9216]{1,0:T(4,128)(2,1)}, f32[3]{0:T(128)}) custom-call(bf16[5,9216]{1,0:T(8,128)(2,1)} %green.1, bf16[8,192,1536]{2,1,0:T(8,128)(2,1)} %chol.1, s32[24]{0:T(128)} %counts.1, s32[2,24]{1,0:T(2,128)} %bitcast.2, s32[2,24]{1,0:T(2,128)} %bitcast.3), custom_call_target="tpu_custom_call" | custom-call | tf_op jit(solution)/shard_map/exchange_energy/pallas_call | solution.py:386
  63.4 1.5 %finish.1 = (bf16[3,9216]{1,0:T(4,128)(2,1)}, f32[3]{0:T(128)}) custom-call(bf16[3,9216]{1,0:T(4,128)(2,1)} %get-tuple-element.4.new_in, f32[3]{0:T(128)} %get-tuple-element.5.en_in), custom_call_target="tpu_custom_call" | custom-call | tf_op jit(solution)/shard_map/finish/pallas_call | solution.py:428

commit v4 on v3

--- a/solution.py
+++ b/solution.py
@@ -296,12 +296,8 @@
     rest(3)
     multiply(2, 0)
     multiply(2, 1)
-    zarrive()
-    for a in range(KEEP):
-        xsend[a] = lbuf[lax.div(other[a], 4), lax.rem(other[a], 2)]
     other_core(3)
     gather_rows(3)
-    send(lambda: xsend, lambda: xrecv, lambda: rx.at[0], dev(y, x, c, z, 1 - yh))
     multiply(3, 0)
     multiply(3, 1)
 
@@ -313,16 +309,25 @@
         value = jnp.sum(jnp.sum(tot, axis=0, keepdims=True), axis=1, keepdims=True)
         part = jnp.where(lane == s, value, part)
 
-    def exchange(buf, sem, me, value, targets, sources):
+    def exchange(buf, sem, me, value, targets, sources, between=None):
         buf[me] = value
         for device in targets:
             both(lambda: buf.at[me], lambda: sem.at[me], device)
+        if between is not None:
+            between()
         for src in sources:
             arrive(buf.at[src], sem.at[src], pd)
+
+    def partner_rows():
+        zarrive()
+        for a in range(KEEP):
+            xsend[a] = lbuf[lax.div(other[a], 4), lax.rem(other[a], 2)]
+        send(lambda: xsend, lambda: xrecv, lambda: rx.at[0], dev(y, x, c, z, 1 - yh))
 
     exchange(
         ea, ra, x * 2 + c, part, xc_peers,
         [lax.rem(x + dx, X) * 2 + cc for dx in range(X) for cc in (c, oc)][1:],
+        partner_rows,
     )
     total = ea[0]
     for i in range(1, 2 * X):

time: 65.7 us -> 65.2 us (level)
  no operation moved by 1% of the time
where the time goes in v4:
time: 65.2 us; the launch traced here: 65 us
  Pallas kernels  64.4 us (99%)
    pallas_call x1, Pallas kernels, body(): pl.pallas_call(kernel, out_shape=(jax.ShapeDtypeStruct((KEEP, SHARE), BF)...  62.9 us
    pallas_call x1, Pallas kernels, body(): pl.pallas_call(finish, out_shape=(jax.ShapeDtypeStruct((KEEP, SHARE), BF)...  1.55 us

profile of v4, /device:TPU:1, one launch (start us, length us, event | category | flops | bytes accessed | tf_op | source)
XLA Modules:
  0.0 65.0 jit_solution(12948615478167016630)
XLA Ops:
  0.6 62.9 %exchange_energy.1 = (bf16[3,9216]{1,0:T(4,128)(2,1)}, f32[3]{0:T(128)}) custom-call(bf16[5,9216]{1,0:T(8,128)(2,1)} %green.1, bf16[8,192,1536]{2,1,0:T(8,128)(2,1)} %chol.1, s32[24]{0:T(128)} %counts.1, s32[2,24]{1,0:T(2,128)} %bitcast.2, s32[2,24]{1,0:T(2,128)} %bitcast.3), custom_call_target="tpu_custom_call" | custom-call | tf_op jit(solution)/shard_map/exchange_energy/pallas_call | solution.py:391
  63.5 1.5 %finish.1 = (bf16[3,9216]{1,0:T(4,128)(2,1)}, f32[3]{0:T(128)}) custom-call(bf16[3,9216]{1,0:T(4,128)(2,1)} %get-tuple-element.4.new_in, f32[3]{0:T(128)} %get-tuple-element.5.en_in), custom_call_target="tpu_custom_call" | custom-call | tf_op jit(solution)/shard_map/finish/pallas_call | solution.py:433
